TPU v7x, 32 devices: a whole 2x2x4 slice. The times are simulated.
32 devices in a mesh: dp: 8 (over z, x), expert: 4 (over y, core).
Axes of the slice: x: 2, y: 2, z: 4, core: 2. Of those that a mesh axis runs over, the one named last changes fastest.
Arguments:
- tokens: bfloat16 [4096, 2048], P(('dp', 'expert')), may hold values from -6 to 6
- d_out: bfloat16 [4096, 2048], P(('dp', 'expert')), may hold values from -6 to 6
- routes: int32 [4096, 2], P(('dp', 'expert')), may hold values from 0 to 3, all different within a row; in each aligned block of 128 rows (0 to 127, 128 to 255, ...) at most 96 rows name the same one
- gate_fixed: int32 [4096, 2], P(('dp', 'expert')), may hold values from 1 to 65535
- w_gate: bfloat16 [4, 2048, 768], P('expert'), may hold values from -0.125 to 0.125
- w_up: bfloat16 [4, 2048, 768], P('expert'), may hold values from -0.125 to 0.125
- w_down: bfloat16 [4, 768, 2048], P('expert'), may hold values from -0.21875 to 0.21875
Outputs:
- d_tokens: bfloat16 [4096, 2048], P(('dp', 'expert'))
- d_wgate: float32 [4, 2048, 768], P('expert', 'dp')
- d_wup: float32 [4, 2048, 768], P('expert', 'dp')
- d_wdown: float32 [4, 768, 2048], P('expert', 'dp')
Inputs may be any that keep to these rules, and one draw needn't show every extreme that they name: Each token names 2 different experts; of the routes of one device's 128 tokens (aligned blocks of rows) at most 96 name any one expert, a bound that some block reaches of them.
All inputs are finite; a program needn't handle non-finite values.
Results may differ from a plain program's by a relative error of at most 0.0065.
Values may be sent and summed in bfloat16 or wider, within the bound.
A program may use at most 192 MiB of HBM per device.

v0:
```python
import jax
import jax.numpy as jnp
from jax import lax
from jax.sharding import PartitionSpec as P


def forward_part(rows_x, w_gate, w_up):
    pre_gate = jnp.einsum("erd,edi->eri", rows_x, w_gate, preferred_element_type=jnp.float32)
    pre_up = jnp.einsum("erd,edi->eri", rows_x, w_up, preferred_element_type=jnp.float32)
    return (pre_gate, pre_up)


def backward_part(pre_gate, pre_up, scaled, w_gate, w_up, w_down):
    sigmoid_gate = jax.nn.sigmoid(pre_gate)
    silu_gate = pre_gate * sigmoid_gate
    hidden = (silu_gate * pre_up).astype(jnp.bfloat16)
    d_hidden = jnp.einsum("erd,eid->eri", scaled, w_down, preferred_element_type=jnp.float32)
    d_gate = (d_hidden * pre_up * sigmoid_gate * (1.0 + pre_gate * (1.0 - sigmoid_gate))).astype(
        jnp.bfloat16
    )
    d_up = (d_hidden * silu_gate).astype(jnp.bfloat16)
    route_grad = (
        jnp.einsum("eri,edi->erd", d_gate, w_gate, preferred_element_type=jnp.float32)
        + jnp.einsum("eri,edi->erd", d_up, w_up, preferred_element_type=jnp.float32)
    ).astype(jnp.bfloat16)
    return (hidden, d_gate, d_up, route_grad)


def body(tokens, d_out, routes, gate_fixed, w_gate, w_up, w_down):
    expert_span = lax.axis_size("expert")
    replicas = lax.axis_size("dp")
    local_count = w_gate.shape[0]
    expert_total = expert_span * local_count
    token_count, top_count = routes.shape
    model_width = tokens.shape[1]
    hidden_units = w_gate.shape[2]
    capacity = 3 * token_count * top_count // (2 * expert_total)
    inverse = 1.0 / replicas
    expert_ids = routes.reshape(-1)
    one_hot = (expert_ids[:, None] == jnp.arange(expert_total, dtype=jnp.int32)[None, :]).astype(
        jnp.int32
    )
    earlier = jnp.cumsum(one_hot, axis=0) - one_hot
    slot_index = jnp.sum(earlier * one_hot, axis=1)
    target = expert_ids * capacity + slot_index
    placing = (
        target[:, None] == jnp.arange(expert_total * capacity, dtype=jnp.int32)[None, :]
    ).astype(jnp.bfloat16)
    token_placing = jnp.sum(placing.reshape(token_count, top_count, -1), axis=1)
    gate_value = gate_fixed.astype(jnp.float32) / 65536.0
    scaled_routes = (gate_value[:, :, None] * d_out[:, None, :].astype(jnp.float32)).astype(
        jnp.bfloat16
    )
    scaled_routes = scaled_routes.reshape(-1, model_width)
    send_x = jnp.einsum("ts,td->sd", token_placing, tokens, preferred_element_type=jnp.float32)
    send_x = send_x.astype(jnp.bfloat16).reshape(expert_total, capacity, model_width)
    send_scaled = jnp.einsum(
        "rs,rd->sd", placing, scaled_routes, preferred_element_type=jnp.float32
    )
    send_scaled = send_scaled.astype(jnp.bfloat16).reshape(expert_total, capacity, model_width)
    rows_x, scaled = (
        lax.all_to_all(send_x, "expert", split_axis=0, concat_axis=1, tiled=True),
        lax.all_to_all(send_scaled, "expert", split_axis=0, concat_axis=1, tiled=True),
    )
    pre_gate, pre_up = forward_part(rows_x, w_gate, w_up)
    hidden, d_gate, d_up, route_grad = backward_part(pre_gate, pre_up, scaled, w_gate, w_up, w_down)
    returned = lax.all_to_all(route_grad, "expert", split_axis=1, concat_axis=0, tiled=True)
    route_rows = jnp.einsum(
        "rs,sd->rd", placing, returned.reshape(-1, model_width), preferred_element_type=jnp.float32
    )
    d_tokens = jnp.sum(route_rows.reshape(token_count, top_count, model_width), axis=1).astype(
        jnp.bfloat16
    )
    stacked = jnp.concatenate([d_gate, d_up], axis=2)
    feature_rows = model_width // replicas
    split_rows = rows_x.reshape(local_count, rows_x.shape[1], replicas, feature_rows)
    columns = lax.all_to_all(split_rows, "dp", split_axis=2, concat_axis=1, tiled=True)
    columns = columns.reshape(local_count, -1, feature_rows)
    reduced = (
        jnp.einsum(
            "erc,erj->cej",
            columns,
            lax.all_gather(stacked, "dp", axis=1, tiled=True),
            preferred_element_type=jnp.float32,
        )
        * inverse
    )
    d_wgate = jnp.transpose(reduced[:, :, :hidden_units], (1, 0, 2))
    d_wup = jnp.transpose(reduced[:, :, hidden_units:], (1, 0, 2))
    down_reduced = lax.psum_scatter(
        jnp.einsum("erc,erd->ced", hidden, scaled, preferred_element_type=jnp.float32) * inverse,
        "dp",
        scatter_dimension=0,
        tiled=True,
    )
    d_wdown = jnp.transpose(down_reduced, (1, 0, 2))
    return (d_tokens, d_wgate, d_wup, d_wdown)


def solution(mesh):
    in_specs = (
        P(("dp", "expert"), None),
        P(("dp", "expert"), None),
        P(("dp", "expert"), None),
        P(("dp", "expert"), None),
        P("expert", None, None),
        P("expert", None, None),
        P("expert", None, None),
    )
    out_specs = (
        P(("dp", "expert"), None),
        P("expert", "dp", None),
        P("expert", "dp", None),
        P("expert", "dp", None),
    )
    return jax.shard_map(body, mesh=mesh, in_specs=in_specs, out_specs=out_specs, check_vma=False)
```

profile of v0, /device:TPU:0, one launch (start us, length us, event | category | flops | bytes accessed | tf_op | source)
XLA Modules:
  0.0 478.5 jit_solution(15510985037377215370)
XLA Ops:
  7.2 0.0 copy-start
  7.2 0.9 copy.83
  8.1 0.1 eq.71
  8.3 0.1 eq.67
  8.4 1.2 reduce-window.6
  9.6 0.1 slice.16
  9.7 0.1 copy.85
  9.9 0.1 copy.86
  10.0 0.1 add_bitcast_fusion
  10.1 0.1 reduce_sum.33
  10.2 0.1 copy.87
  10.3 0.7 multiply_add_fusion.1
  11.0 0.1 fusion.35
  11.1 2.8 convolution_convert_fusion
  13.9 4.4 all-to-all-start.1
  18.3 3.4 mul.95
  21.7 3.7 mul.96
  25.4 0.0 copy-done.5
  25.4 0.1 copy.88
  25.5 0.1 mul.93
  25.7 3.4 convolution_convert_fusion.1
  29.1 10.0 %all-to-all-done.1 = bf16[4,96,2048]{2,1,0:T(8,128)(2,1)} async-done(((bf16[4,96,2048]{2,1,0:T(8,128)(2,1)}), bf16[4,96,2048]{2,1,0:T(8,128)(2,1)}, u32[]{:S(2)}, u32[]{:S(2)}) %all-to-all-start.1) | async-done | bytes 1572896 | tf_op jit(solution)/shard_map/all_to_all | solution.py:62
  39.0 4.4 all-to-all-start
  43.4 0.0 all-reduce.3.cloned.1.call-start
  43.5 0.0 copy-start.6
  43.5 4.1 fusion.4
  47.6 3.8 fusion.8
  51.4 12.2 %all-to-all-done = bf16[4,96,2048]{2,1,0:T(8,128)(2,1)} async-done(((bf16[4,96,2048]{2,1,0:T(8,128)(2,1)}), bf16[4,96,2048]{2,1,0:T(8,128)(2,1)}, u32[]{:S(2)}, u32[]{:S(2)}) %all-to-all-start) | async-done | bytes 1572896 | tf_op jit(solution)/shard_map/all_to_all | solution.py:63
  63.6 6.7 %multiply_bitcast_fusion = f32[768,1,2048]{0,2,1:T(8,128)} fusion(bf16[384,2048]{1,0:T(8,128)(2,1)} %bitcast.4, f32[384,768]{1,0:T(8,128)} %fusion.8, f32[384,768]{1,0:T(8,128)} %fusion.4), kind=kOutput, calls=%fused_computation.2 | convolution fusion | flops 1211301888 | bytes 10223616 | tf_op jit(solution)/shard_map/erc,erd->ced/dot_general | solution.py:91
  70.2 15.9 %copy.91 = f32[768,1,2048]{2,1,0:T(1,128)} copy(f32[768,1,2048]{0,2,1:T(8,128)} %multiply_bitcast_fusion) | data formatting | bytes 12582912 | tf_op jit(solution)/shard_map/mul | solution.py:91
  86.2 0.0 all-reduce.3.cloned.1.call-update
  86.2 0.2 all-gather.2.cloned.1.call-start
  86.4 4.7 multiply_convert_fusion.2
  91.2 0.0 copy-start.2
  91.2 0.0 copy-start.4
  91.2 0.8 copy-done.2
  92.0 0.2 copy-done.4
  92.2 1.1 pad_maximum_fusion
  93.3 0.0 all-gather.2.cloned.1.call-update
  93.3 0.0 copy-start.3
  93.3 0.0 copy-start.7
  93.3 2.6 fusion.2
  96.0 1.4 fusion.20
  97.4 2.4 copy.106
  99.9 0.5 broadcast.74
  100.4 11.3 %reduce.1 = bf16[384,2048]{1,0:T(8,128)(2,1)} reduce(bf16[384,1,2048]{2,1,0:T(2,128)(2,1)S(1)} %bitcast.98, bf16[]{:T(256)} %broadcast.74), dimensions={1}, to_apply=%bitcast.97.reduce_sub_computation | reduce | bytes 3145730
  111.7 4.2 reshape.180
  115.9 3.6 all-to-all-start.2
  119.4 1.9 copy.97
  121.4 1.5 copy.90
  122.8 16.7 %all-to-all-done.2 = bf16[4,2,98304]{2,1,0:T(2,128)(2,1)S(1)} async-done(((bf16[4,2,98304]{2,1,0:T(2,128)(2,1)}), bf16[4,2,98304]{2,1,0:T(2,128)(2,1)S(1)}, u32[]{:S(2)}, u32[]{:S(2)}) %all-to-all-start.2) | async-done | bytes 1572896 | tf_op jit(solution)/shard_map/all_to_all | solution.py:67
  139.5 6.6 %all-to-all-start.3 = ((bf16[1,384,8,256]{3,1,0,2:T(8,128)(2,1)}), bf16[1,384,8,256]{3,1,0,2:T(8,128)(2,1)}, u32[]{:S(2)}, u32[]{:S(2)}) async-start(bf16[1,384,8,256]{3,1,0,2:T(8,128)(2,1)} %copy.90), calls=%async_computation.3 | async-start | bytes 3145728 | tf_op jit(solution)/shard_map/all_to_all | solution.py:77
  146.1 0.6 dynamic-slice
  147.3 2.9 reshape.181
  150.2 4.0 fusion.26
  154.2 166.2 %all-reduce.3.cloned.1.call-done = f32[768,1,2048]{2,1,0:T(1,128)} async-done(((f32[768,1,2048]{2,1,0:T(1,128)}), f32[768,1,2048]{2,1,0:T(1,128)}) %all-reduce.3.cloned.1.call-update) | async-done | bytes 6291472
  320.5 1.2 dynamic-slice_bitcast_fusion
  321.7 1.1 copy.94
  322.8 0.0 all-to-all-done.3
  322.8 137.2 %all-gather.2.cloned.1.call-done = bf16[1,3072,1536]{2,1,0:T(8,128)(2,1)} async-done(((bf16[1,384,1536]{2,1,0:T(8,128)(2,1)}), bf16[1,3072,1536]{2,1,0:T(8,128)(2,1)}) %all-gather.2.cloned.1.call-update) | async-done | bytes 9437200 | tf_op jit(solution)/shard_map/all_gather | solution.py:83
  460.0 5.7 %fusion.17 = f32[256,1,1536]{0,2,1:T(8,128)S(1)} fusion(bf16[3072,256]{1,0:T(8,128)(2,1)} %bitcast.16, bf16[1,3072,1536]{2,1,0:T(8,128)(2,1)} %all-gather.2.cloned.1.call-done), kind=kOutput, calls=%fused_computation.17 | convolution fusion | flops 2416312320 | bytes 12582912 | tf_op jit(solution)/shard_map/erc,erj->cej/dot_general | solution.py:80
  465.7 1.2 slice_bitcast_fusion
  466.9 2.4 copy.92
  469.4 2.3 copy.93
  (15 shorter events, 0.1 us)
Async XLA Ops:
  7.2 36.3 %copy-start = (bf16[1,2048,768]{2,1,0:T(8,128)(2,1)S(1)}, bf16[1,2048,768]{2,1,0:T(8,128)(2,1)}, u32[]{:S(2)}) copy-start(bf16[1,2048,768]{2,1,0:T(8,128)(2,1)} %param.11) | copy-start | bytes 9437188
  13.9 25.1 %all-to-all-start.1 = ((bf16[4,96,2048]{2,1,0:T(8,128)(2,1)}), bf16[4,96,2048]{2,1,0:T(8,128)(2,1)}, u32[]{:S(2)}, u32[]{:S(2)}) async-start(bf16[4,96,2048]{2,1,0:T(8,128)(2,1)} %bitcast.99), calls=%async_computation.1 | async-start | bytes 3145728 | tf_op jit(solution)/shard_map/all_to_all | solution.py:62
  21.7 3.7 copy-start.5
  39.0 24.5 %all-to-all-start = ((bf16[4,96,2048]{2,1,0:T(8,128)(2,1)}), bf16[4,96,2048]{2,1,0:T(8,128)(2,1)}, u32[]{:S(2)}, u32[]{:S(2)}) async-start(bf16[4,96,2048]{2,1,0:T(8,128)(2,1)} %bitcast.100), calls=%async_computation | async-start | bytes 3145728 | tf_op jit(solution)/shard_map/all_to_all | solution.py:63
  43.4 277.1 %all-reduce.3.cloned.1.call-start = ((), (), s32[]{:S(2)}) async-start(), calls=%async_computation.5 | async-start | bytes 12582912
  43.5 4.1 copy-start.6
  86.2 373.8 %all-gather.2.cloned.1.call-start = ((), (), s32[]{:S(2)}) async-start(), calls=%async_computation.4 | async-start | bytes 10616832 | tf_op jit(solution)/shard_map/all_gather | solution.py:83
  91.2 0.8 copy-start.2
  91.2 1.0 copy-start.4
  93.3 2.7 copy-start.3
  93.3 2.7 copy-start.7
  115.9 23.6 %all-to-all-start.2 = ((bf16[4,2,98304]{2,1,0:T(2,128)(2,1)}), bf16[4,2,98304]{2,1,0:T(2,128)(2,1)S(1)}, u32[]{:S(2)}, u32[]{:S(2)}) async-start(bf16[4,2,98304]{2,1,0:T(2,128)(2,1)} %reshape.180), calls=%async_computation.2 | async-start | bytes 3145728 | tf_op jit(solution)/shard_map/all_to_all | solution.py:67
  122.8 23.3 %copy-start.8 = (u32[32]{0:T(128)S(1)}, u32[32]{0:T(128)}, u32[]{:S(2)}) copy-start(u32[32]{0:T(128)} %constant.25) | copy-start | bytes 388
  139.5 183.3 %all-to-all-start.3 = ((bf16[1,384,8,256]{3,1,0,2:T(8,128)(2,1)}), bf16[1,384,8,256]{3,1,0,2:T(8,128)(2,1)}, u32[]{:S(2)}, u32[]{:S(2)}) async-start(bf16[1,384,8,256]{3,1,0,2:T(8,128)(2,1)} %copy.90), calls=%async_computation.3 | async-start | bytes 3145728 | tf_op jit(solution)/shard_map/all_to_all | solution.py:77
  466.9 4.7 copy-start.1
Sparse Core Ops, SparseCore 0:
  86.3 234.1 all-reduce.2
  322.9 137.0 all-gather.1
where the time goes:
time: 480 us; the launch traced here: 478 us
  waiting for transfers between devices  342 us (71%)
  local copies, waits for them, and re-layouts  48.2 us (10%)
  matrix products  39.4 us (8%)
  starting transfers between devices  19.1 us (4%)
  between operations  14.9 us (3%)
  other arithmetic  14.6 us (3%)
    unnamed x3, waiting for transfers between devices  166 us
    all_gather x1, waiting for transfers between devices, body(): lax.all_gather(stacked, 'dp', axis=1, tiled=True)  137 us
    unnamed x27, local copies, waits for them, and re-layouts  17.9 us
    all_to_all x1, waiting for transfers between devices, body(): lax.all_to_all(route_grad, 'expert', split_axis=1, concat_axis=0, tiled=T...  16.7 us
    mul x1, local copies, waits for them, and re-layouts, body(): jnp.einsum('erc,erd->ced', hidden, scaled, preferred_element_type=jnp.flo...  15.9 us
    all_to_all x1, waiting for transfers between devices, body(): lax.all_to_all(send_scaled, 'expert', split_axis=0, concat_axis=1, tiled=...  12.2 us
    unnamed x2, other arithmetic  11.4 us
    all_to_all x1, waiting for transfers between devices, body(): lax.all_to_all(send_x, 'expert', split_axis=0, concat_axis=1, tiled=True)  9.95 us
  transfers between devices with their start and end apart: 6, of which 5 were waited for; matrix products, arithmetic and copies ran while one was open for 13% of the time, Pallas kernels for 0%

commit v1 on v0

--- a/solution.py
+++ b/solution.py
@@ -76,12 +76,35 @@
     split_rows = rows_x.reshape(local_count, rows_x.shape[1], replicas, feature_rows)
     columns = lax.all_to_all(split_rows, "dp", split_axis=2, concat_axis=1, tiled=True)
     columns = columns.reshape(local_count, -1, feature_rows)
+
+    def _trace_loads(base_x, patch):
+        odd = jax.lax.axis_size("dp")
+        current_value = jax.lax.axis_index("dp")
+        field_out, current_block, k_now = (odd, current_value, base_x.shape[1])
+        pool = [(ix, (ix + 1) % field_out) for ix in range(field_out)]
+        stack_in = [(ix, (ix - 1) % field_out) for ix in range(field_out)]
+        current_arr = field_out // 2
+        fresh = prior = base_x
+        block_now = patch(base_x, current_block * k_now)
+        for dd in range(1, current_arr + 1):
+            fresh = jax.lax.ppermute(fresh, axis_name="dp", perm=pool)
+            if dd < field_out - current_arr:
+                prior = jax.lax.ppermute(prior, axis_name="dp", perm=stack_in)
+                heard = patch(prior, (current_block + dd) % field_out * k_now)
+                block_now = block_now + heard
+            high = patch(fresh, (current_block - dd) % field_out * k_now)
+            block_now = block_now + high
+        return block_now
+
     reduced = (
-        jnp.einsum(
-            "erc,erj->cej",
-            columns,
-            lax.all_gather(stacked, "dp", axis=1, tiled=True),
-            preferred_element_type=jnp.float32,
+        _trace_loads(
+            stacked,
+            lambda own_block, at: jnp.einsum(
+                "erc,erj->cej",
+                lax.dynamic_slice_in_dim(columns, at, own_block.shape[1], axis=1),
+                own_block,
+                preferred_element_type=jnp.float32,
+            ),
         )
         * inverse
     )

time: 480 us -> 481 us (level)
  waiting for transfers between devices: 342 us -> 319 us
  starting transfers between devices: 19.1 us -> 36.9 us
  matrix products: 39.4 us -> 44.8 us
    ppermute x0 -> x7, waiting for transfers between devices: none -> 229 us  [the longest x4 229 us: _trace_loads(): fresh = jax.lax.ppermute(fresh, axis_name='dp', perm=pool)]
    all_gather x1 -> x0, waiting for transfers between devices: 137 us -> none  [body(): lax.all_gather(stacked, 'dp', axis=1, tiled=True)]
    unnamed x3 -> x2, waiting for transfers between devices: 166 us -> 67.5 us
    ppermute x0 -> x7, starting transfers between devices: none -> 17.6 us  [the longest x3 10.5 us: _trace_loads(): prior = jax.lax.ppermute(prior, axis_name='dp', perm=stack_in)]
    all_to_all x1, waiting for transfers between devices: 16.7 us -> 0.01 us  [body(): lax.all_to_all(route_grad, 'expert', split_axis=1, concat_axis=0, tiled=T...]
    dot_general x1 -> x8, matrix products: 5.71 us -> 12.9 us  [body(): jnp.einsum('erc,erj->cej', lax.dynamic_slice_in_dim(columns, at, own_bloc...]
    unnamed x27 -> x35, local copies, waits for them, and re-layouts: 17.9 us -> 18.8 us
  transfers between devices with their start and end apart: 6 -> 12, of which waited for: 5 -> 7; matrix products, arithmetic and copies ran while one was open for 13% -> 15% of each run, Pallas kernels for 0% -> 0%
where the time goes in v1:
time: 481 us; the launch traced here: 479 us
  waiting for transfers between devices  319 us (66%)
  local copies, waits for them, and re-layouts  49 us (10%)
  matrix products  44.8 us (9%)
  starting transfers between devices  36.9 us (8%)
  between operations  15 us (3%)
  other arithmetic  14.7 us (3%)
    ppermute x4, waiting for transfers between devices, _trace_loads(): fresh = jax.lax.ppermute(fresh, axis_name='dp', perm=pool)  229 us
    unnamed x2, waiting for transfers between devices  67.5 us
    unnamed x35, local copies, waits for them, and re-layouts  18.8 us
    mul x1, local copies, waits for them, and re-layouts, body(): jnp.einsum('erc,erd->ced', hidden, scaled, preferred_element_type=jnp.flo...  16 us
    dot_general x8, matrix products, body(): jnp.einsum('erc,erj->cej', lax.dynamic_slice_in_dim(columns, at, own_bloc...  12.9 us
    all_to_all x1, waiting for transfers between devices, body(): lax.all_to_all(send_scaled, 'expert', split_axis=0, concat_axis=1, tiled=...  12.1 us
    unnamed x2, other arithmetic  11.3 us
    ppermute x3, starting transfers between devices, _trace_loads(): prior = jax.lax.ppermute(prior, axis_name='dp', perm=stack_in)  10.5 us
  transfers between devices with their start and end apart: 12, of which 7 were waited for; matrix products, arithmetic and copies ran while one was open for 15% of the time, Pallas kernels for 0%

profile of v1, /device:TPU:0, one launch (start us, length us, event | category | flops | bytes accessed | tf_op | source)
XLA Modules:
  0.0 479.1 jit_solution(14544963493512185925)
XLA Ops:
  7.2 0.9 copy.83
  8.1 0.1 eq.79
  8.3 0.1 eq.75
  8.4 1.2 reduce-window.6
  9.7 0.1 copy.85
  10.1 0.1 reduce_sum.33
  10.3 0.7 multiply_add_fusion.1
  11.0 0.1 fusion.42
  11.1 2.8 convolution_convert_fusion
  13.9 4.4 all-to-all-start.1
  18.3 3.4 mul.113
  21.7 3.7 mul.114
  25.4 0.1 copy.88
  25.5 0.1 mul.111
  25.6 3.5 convolution_convert_fusion.1
  29.1 9.9 %all-to-all-done.1 = bf16[4,96,2048]{2,1,0:T(8,128)(2,1)} async-done(((bf16[4,96,2048]{2,1,0:T(8,128)(2,1)}), bf16[4,96,2048]{2,1,0:T(8,128)(2,1)}, u32[]{:S(2)}, u32[]{:S(2)}) %all-to-all-start.1) | async-done | bytes 1572896 | tf_op jit(solution)/shard_map/all_to_all | solution.py:62
  39.0 4.5 all-to-all-start
  43.6 4.0 fusion.2
  47.6 3.8 fusion.6
  51.4 12.1 %all-to-all-done = bf16[4,96,2048]{2,1,0:T(8,128)(2,1)} async-done(((bf16[4,96,2048]{2,1,0:T(8,128)(2,1)}), bf16[4,96,2048]{2,1,0:T(8,128)(2,1)}, u32[]{:S(2)}, u32[]{:S(2)}) %all-to-all-start) | async-done | bytes 1572896 | tf_op jit(solution)/shard_map/all_to_all | solution.py:63
  63.5 4.7 multiply_convert_fusion.2
  68.3 1.4 fusion
  69.7 0.9 copy-done.10
  70.6 1.4 fusion.16
  72.0 2.4 copy.106
  74.4 0.5 broadcast.82
  74.9 11.2 %reduce.1 = bf16[384,2048]{1,0:T(8,128)(2,1)} reduce(bf16[384,1,2048]{2,1,0:T(2,128)(2,1)S(1)} %bitcast.138, bf16[]{:T(256)} %broadcast.82), dimensions={1}, to_apply=%bitcast.137.reduce_sub_computation | reduce | bytes 3145730
  86.2 4.1 reshape.252
  90.3 3.7 all-to-all-start.2
  94.1 6.3 %multiply_bitcast_fusion = f32[768,1,2048]{0,2,1:T(8,128)} fusion(bf16[384,2048]{1,0:T(8,128)(2,1)} %bitcast.4, f32[384,768]{1,0:T(8,128)} %fusion.6, f32[384,768]{1,0:T(8,128)S(1)} %copy-done.12), kind=kOutput, calls=%fused_computation | convolution fusion | flops 1211301888 | bytes 10223616 | tf_op jit(solution)/shard_map/erc,erd->ced/dot_general | solution.py:114
  100.4 16.0 %copy.91 = f32[768,1,2048]{2,1,0:T(1,128)} copy(f32[768,1,2048]{0,2,1:T(8,128)} %multiply_bitcast_fusion) | data formatting | bytes 12582912 | tf_op jit(solution)/shard_map/mul | solution.py:114
  116.4 1.9 copy.97
  118.3 1.5 copy.90
  119.7 6.6 %all-to-all-start.3 = ((bf16[1,384,8,256]{3,1,0,2:T(8,128)(2,1)}), bf16[1,384,8,256]{3,1,0,2:T(8,128)(2,1)S(1)}, u32[]{:S(2)}, u32[]{:S(2)}) async-start(bf16[1,384,8,256]{3,1,0,2:T(8,128)(2,1)} %copy.90), calls=%async_computation.3 | async-start | bytes 3145728 | tf_op jit(solution)/shard_map/all_to_all | solution.py:77
  126.4 1.3 pad_maximum_fusion
  127.7 2.1 collective-permute-start.1
  129.8 2.8 collective-permute-start
  132.5 101.1 %collective-permute-done.1 = bf16[1,384,1536]{2,1,0:T(8,128)(2,1)S(1)} collective-permute-done((bf16[1,384,1536]{2,1,0:T(8,128)(2,1)S(1)}, bf16[1,384,1536]{2,1,0:T(8,128)(2,1)S(1)}, u32[]{:S(2)}, u32[]{:S(2)}) %collective-permute-start.1) | collective-permute-done | bytes 1179680 | tf_op jit(solution)/shard_map/ppermute | solution.py:90
  233.6 1.0 copy-done.4
  234.7 4.7 collective-permute-start.2
  239.4 45.5 %collective-permute-done.3 = bf16[1,384,1536]{2,1,0:T(8,128)(2,1)} collective-permute-done((bf16[1,384,1536]{2,1,0:T(8,128)(2,1)S(1)}, bf16[1,384,1536]{2,1,0:T(8,128)(2,1)}, u32[]{:S(2)}, u32[]{:S(2)}) %collective-permute-start.3) | collective-permute-done | bytes 1179680 | tf_op jit(solution)/shard_map/ppermute | solution.py:90
  284.9 2.6 collective-permute-start.5
  287.5 0.6 dynamic-slice
  288.7 2.9 reshape.253
  291.6 4.0 fusion.22
  295.6 3.0 collective-permute-start.4
  298.6 1.2 copy-done.2
  299.8 1.9 fusion.34
  301.6 2.0 convolution_add_fusion.4
  303.8 0.6 convolution_add_fusion.3
  304.4 44.0 %collective-permute-done.5 = bf16[1,384,1536]{2,1,0:T(8,128)(2,1)} collective-permute-done((bf16[1,384,1536]{2,1,0:T(8,128)(2,1)}, bf16[1,384,1536]{2,1,0:T(8,128)(2,1)}, u32[]{:S(2)}, u32[]{:S(2)}) %collective-permute-start.5) | collective-permute-done | bytes 1179680 | tf_op jit(solution)/shard_map/ppermute | solution.py:90
  348.4 2.5 collective-permute-start.6
  350.9 1.9 fusion.29
  352.8 2.0 fusion.14
  354.8 1.9 fusion.26
  356.7 2.0 fusion.13
  358.7 38.5 %collective-permute-done.6 = bf16[1,384,1536]{2,1,0:T(8,128)(2,1)S(1)} collective-permute-done((bf16[1,384,1536]{2,1,0:T(8,128)(2,1)}, bf16[1,384,1536]{2,1,0:T(8,128)(2,1)S(1)}, u32[]{:S(2)}, u32[]{:S(2)}) %collective-permute-start.6) | collective-permute-done | bytes 1179680 | tf_op jit(solution)/shard_map/ppermute | solution.py:90
  397.2 0.6 fusion.15
  397.9 1.0 slice_bitcast_fusion
  398.8 1.1 copy.92
  400.0 2.5 copy.93
  402.4 67.5 %all-reduce.3.cloned.1.call-done = f32[768,1,2048]{2,1,0:T(1,128)} async-done(((f32[768,1,2048]{2,1,0:T(1,128)}), f32[768,1,2048]{2,1,0:T(1,128)}) %all-reduce.3.cloned.1.call-update) | async-done | bytes 6291472
  470.0 1.2 dynamic-slice_bitcast_fusion
  471.1 1.1 copy.94
  (41 shorter events, 0.6 us)
Async XLA Ops:
  7.2 36.4 %copy-start = (bf16[1,2048,768]{2,1,0:T(8,128)(2,1)S(1)}, bf16[1,2048,768]{2,1,0:T(8,128)(2,1)}, u32[]{:S(2)}) copy-start(bf16[1,2048,768]{2,1,0:T(8,128)(2,1)} %param.11) | copy-start | bytes 9437188
  13.9 25.1 %all-to-all-start.1 = ((bf16[4,96,2048]{2,1,0:T(8,128)(2,1)}), bf16[4,96,2048]{2,1,0:T(8,128)(2,1)}, u32[]{:S(2)}, u32[]{:S(2)}) async-start(bf16[4,96,2048]{2,1,0:T(8,128)(2,1)} %bitcast.139), calls=%async_computation.1 | async-start | bytes 3145728 | tf_op jit(solution)/shard_map/all_to_all | solution.py:62
  21.7 3.7 copy-start.8
  39.0 24.5 %all-to-all-start = ((bf16[4,96,2048]{2,1,0:T(8,128)(2,1)}), bf16[4,96,2048]{2,1,0:T(8,128)(2,1)}, u32[]{:S(2)}, u32[]{:S(2)}) async-start(bf16[4,96,2048]{2,1,0:T(8,128)(2,1)} %bitcast.140), calls=%async_computation | async-start | bytes 3145728 | tf_op jit(solution)/shard_map/all_to_all | solution.py:63
  43.6 4.0 copy-start.9
  68.2 1.5 copy-start.7
  68.2 1.5 copy-start.6
  68.2 2.3 copy-start.10
  90.3 3.8 copy-start.12
  90.3 29.4 %all-to-all-start.2 = ((bf16[4,2,98304]{2,1,0:T(2,128)(2,1)}), bf16[4,2,98304]{2,1,0:T(2,128)(2,1)S(1)}, u32[]{:S(2)}, u32[]{:S(2)}) async-start(bf16[4,2,98304]{2,1,0:T(2,128)(2,1)} %reshape.252), calls=%async_computation.2 | async-start | bytes 3145728 | tf_op jit(solution)/shard_map/all_to_all | solution.py:67
  94.0 376.0 %all-reduce.3.cloned.1.call-start = ((), (), s32[]{:S(2)}) async-start(), calls=%async_computation.4 | async-start | bytes 12582912
  119.7 178.9 %all-to-all-start.3 = ((bf16[1,384,8,256]{3,1,0,2:T(8,128)(2,1)}), bf16[1,384,8,256]{3,1,0,2:T(8,128)(2,1)S(1)}, u32[]{:S(2)}, u32[]{:S(2)}) async-start(bf16[1,384,8,256]{3,1,0,2:T(8,128)(2,1)} %copy.90), calls=%async_computation.3 | async-start | bytes 3145728 | tf_op jit(solution)/shard_map/all_to_all | solution.py:77
  126.4 161.1 %copy-start.11 = (u32[32]{0:T(128)S(1)}, u32[32]{0:T(128)}, u32[]{:S(2)}) copy-start(u32[32]{0:T(128)} %constant.86) | copy-start | bytes 388
  127.7 105.9 %collective-permute-start.1 = (bf16[1,384,1536]{2,1,0:T(8,128)(2,1)S(1)}, bf16[1,384,1536]{2,1,0:T(8,128)(2,1)S(1)}, u32[]{:S(2)}, u32[]{:S(2)}) collective-permute-start(bf16[1,384,1536]{2,1,0:T(8,128)(2,1)S(1)} %pad_maximum_fusion), channel_id=1, source_target_pairs={{0,4},{4,8},{8,12},{12,16},{16,20},{20,24},{24,28},{28,0},{1,5},{5... | collective-permute-start | bytes 3538952 | tf_op jit(solution)/shard_map/ppermute | solution.py:90
  129.8 104.9 %collective-permute-start = (bf16[1,384,1536]{2,1,0:T(8,128)(2,1)S(1)}, bf16[1,384,1536]{2,1,0:T(8,128)(2,1)}, u32[]{:S(2)}, u32[]{:S(2)}) collective-permute-start(bf16[1,384,1536]{2,1,0:T(8,128)(2,1)S(1)} %pad_maximum_fusion), channel_id=1, source_target_pairs={{0,28},{4,0},{8,4},{12,8},{16,12},{20,16},{24,20},{28,24},{1,29},{... | collective-permute-start | bytes 3538952 | tf_op jit(solution)/shard_map/ppermute | solution.py:92
  233.6 1.0 copy-start.4
  234.7 50.3 %collective-permute-start.3 = (bf16[1,384,1536]{2,1,0:T(8,128)(2,1)S(1)}, bf16[1,384,1536]{2,1,0:T(8,128)(2,1)}, u32[]{:S(2)}, u32[]{:S(2)}) collective-permute-start(bf16[1,384,1536]{2,1,0:T(8,128)(2,1)S(1)} %collective-permute-done.1), channel_id=1, source_target_pairs={{0,4},{4,8},{8,12},{12,16},{16,20},{20,24},{24,28},{28,0},{1,5},{5... | collective-permute-start | bytes 3538952 | tf_op jit(solution)/shard_map/ppermute | solution.py:90
  234.7 61.0 %collective-permute-start.2 = (bf16[1,384,1536]{2,1,0:T(8,128)(2,1)}, bf16[1,384,1536]{2,1,0:T(8,128)(2,1)}, u32[]{:S(2)}, u32[]{:S(2)}) collective-permute-start(bf16[1,384,1536]{2,1,0:T(8,128)(2,1)} %collective-permute-done), channel_id=1, source_target_pairs={{0,28},{4,0},{8,4},{12,8},{16,12},{20,16},{24,20},{28,24},{1,29},{... | collective-permute-start | bytes 3538952 | tf_op jit(solution)/shard_map/ppermute | solution.py:92
  284.9 63.5 %collective-permute-start.5 = (bf16[1,384,1536]{2,1,0:T(8,128)(2,1)}, bf16[1,384,1536]{2,1,0:T(8,128)(2,1)}, u32[]{:S(2)}, u32[]{:S(2)}) collective-permute-start(bf16[1,384,1536]{2,1,0:T(8,128)(2,1)} %collective-permute-done.3), channel_id=1, source_target_pairs={{0,4},{4,8},{8,12},{12,16},{16,20},{20,24},{24,28},{28,0},{1,5},{5... | collective-permute-start | bytes 3538952 | tf_op jit(solution)/shard_map/ppermute | solution.py:90
  295.6 61.1 %collective-permute-start.4 = (bf16[1,384,1536]{2,1,0:T(8,128)(2,1)}, bf16[1,384,1536]{2,1,0:T(8,128)(2,1)}, u32[]{:S(2)}, u32[]{:S(2)}) collective-permute-start(bf16[1,384,1536]{2,1,0:T(8,128)(2,1)} %collective-permute-done.2), channel_id=1, source_target_pairs={{0,28},{4,0},{8,4},{12,8},{16,12},{20,16},{24,20},{28,24},{1,29},{... | collective-permute-start | bytes 3538952 | tf_op jit(solution)/shard_map/ppermute | solution.py:92
  298.6 1.2 copy-start.2
  301.6 2.1 copy-start.3
  301.6 2.1 copy-start.5
  348.4 48.8 %collective-permute-start.6 = (bf16[1,384,1536]{2,1,0:T(8,128)(2,1)}, bf16[1,384,1536]{2,1,0:T(8,128)(2,1)S(1)}, u32[]{:S(2)}, u32[]{:S(2)}) collective-permute-start(bf16[1,384,1536]{2,1,0:T(8,128)(2,1)} %collective-permute-done.5), channel_id=1, source_target_pairs={{0,4},{4,8},{8,12},{12,16},{16,20},{20,24},{24,28},{28,0},{1,5},{5... | collective-permute-start | bytes 3538952 | tf_op jit(solution)/shard_map/ppermute | solution.py:90
  400.0 72.3 %copy-start.1 = (bf16[1,2048,768]{2,1,0:T(8,128)(2,1)S(1)}, bf16[1,2048,768]{2,1,0:T(8,128)(2,1)}, u32[]{:S(2)}) copy-start(bf16[1,2048,768]{2,1,0:T(8,128)(2,1)} %param.11) | copy-start | bytes 9437188
Sparse Core Ops, SparseCore 0:
  116.5 353.4 all-reduce.2
